TPU v7x, 256 devices: a whole 4x4x8 slice. The times are simulated.
256 devices in a mesh: seq: 8 (over z_lo, y), outer: 8 (over x, core), inner: 4 (over z_hi).
Axes of the slice: x: 4, y: 4, z: 8 (z_hi: 4, z_lo: 2; z = z_hi * 2 + z_lo), core: 2. Of those that a mesh axis runs over, the one named last changes fastest.
Arguments:
- tokens: bfloat16 [32768, 4096], P(('seq', 'outer', 'inner')), parts along dimension 0, may hold values from -6 to 6
- att_ids: int32 [32768, 2, 2], P(('seq', 'outer', 'inner')), parts along dimension 0, may hold values from 0 to 3, all different within a row
- mlp_ids: int32 [32768, 8], P(('seq', 'outer', 'inner')), parts along dimension 0, may hold values from 0 to 63, all different within a row; in each aligned block of 128 rows (0 to 127, 128 to 255, ...) at most 20 rows name the same one
- att_gain: float32 [4096], replicated, may hold values from 0.25 to 1.75
- att_in: bfloat16 [4096, 768], P('inner'), may hold values from -16 to 16
- att_router: bfloat16 [4096, 8], P('inner'), may hold values from -0.09375 to 0.09375
- att_out: bfloat16 [512, 4096], P(None, 'inner'), may hold values from -0.75 to 0.75
- mlp_gain: float32 [4096], replicated, may hold values from 0.25 to 1.75
- mlp_router: bfloat16 [4096, 64], replicated, may hold values from -0.09375 to 0.09375
- w_up: bfloat16 [64, 4096, 256], P(('outer', 'inner')), may hold values from -0.09375 to 0.09375
- w_down: bfloat16 [64, 256, 4096], P(('outer', 'inner')), may hold values from -0.375 to 0.375
Outputs:
- layer_out: bfloat16 [32768, 4096], P(('seq', 'outer', 'inner')), parts along dimension 0
There are 8 independent parts, one for each index of `seq`. A program takes and returns all parts, laid end to end along the dimension named above; an argument that names none is the same for every part. Nothing has to cross between parts.
Inputs may be any that keep to these rules, and one draw needn't show every extreme that they name: `att_ids`: the 2 ids of one token and head differ. `mlp_ids`: among the rows of one device each expert is named at most 20 times, a bound that some block reaches in some devices' rows.
All inputs are finite; a program needn't handle non-finite values.
Results may differ from a plain program's by a relative error of at most 0.008.
Values may be sent and summed in bfloat16 or wider, within the bound.
A program may use at most 128 MiB of HBM per device.

v0:
```python
import jax
import jax.numpy as jnp
from jax import lax
from jax.sharding import PartitionSpec as P

D = 4096
HEADS = 2
HDIM = 64
ATT_EXP = 4
MLP_TOP = 8
epsilon = 1e-05


def rms_norm(values_in, gain_vector):
    floats = values_in.astype(jnp.float32)
    return (
        floats
        * lax.rsqrt(jnp.mean(floats * floats, axis=-1, keepdims=True) + epsilon)
        * gain_vector
    )


def on_device(
    tokens,
    att_ids,
    mlp_ids,
    att_gain,
    att_in,
    att_router,
    att_out,
    mlp_gain,
    mlp_router,
    w_up,
    w_down,
):
    row_count = tokens.shape[0]
    head_width = HEADS * HDIM
    normed = rms_norm(tokens, att_gain).astype(jnp.bfloat16)
    proj = jnp.dot(
        normed,
        lax.all_gather(att_in, "inner", axis=0, tiled=True),
        preferred_element_type=jnp.float32,
    )
    att_logit = jnp.dot(
        normed,
        lax.all_gather(att_router, "inner", axis=0, tiled=True),
        preferred_element_type=jnp.float32,
    )
    query = proj[:, :head_width].astype(jnp.bfloat16).reshape(row_count, HEADS, HDIM)
    keys = proj[:, head_width : 2 * head_width].astype(jnp.bfloat16)
    value_all = proj[:, 2 * head_width :].reshape(row_count, HEADS, ATT_EXP, HDIM)
    chosen = jnp.sum(
        (att_ids[..., None] == jnp.arange(ATT_EXP)[None, None, None, :]).astype(jnp.float32), axis=2
    )
    att_weight = jax.nn.sigmoid(att_logit.reshape(row_count, HEADS, ATT_EXP)) * chosen
    values = (
        jnp.sum(att_weight[..., None] * value_all, axis=2)
        .astype(jnp.bfloat16)
        .reshape(row_count, head_width)
    )
    first_row = lax.axis_index(("outer", "inner")) * row_count
    query_position = first_row + jnp.arange(row_count)
    score_factor = HDIM ** (-0.5)
    start_state = (
        jnp.full((row_count, HEADS), -1e30, jnp.float32),
        jnp.zeros((row_count, HEADS), jnp.float32),
        jnp.zeros((row_count, HEADS, HDIM), jnp.float32),
    )
    key_piece = lax.all_gather(keys, ("outer", "inner"), axis=0, tiled=True)
    value_piece = lax.all_gather(values, ("outer", "inner"), axis=0, tiled=True)
    piece_rows = key_piece.shape[0]

    def update(current):
        running_max, running_sum, accumulated = current
        key_heads = key_piece.reshape(piece_rows, HEADS, HDIM)
        value_heads = value_piece.reshape(piece_rows, HEADS, HDIM).astype(jnp.float32)
        scores = (
            jnp.einsum("thd,shd->ths", query, key_heads, preferred_element_type=jnp.float32)
            * score_factor
        )
        key_position = jnp.arange(piece_rows)
        visible = key_position[None, None, :] <= query_position[:, None, None]
        scores = jnp.where(visible, scores, -1e30)
        new_max = jnp.maximum(running_max, jnp.max(scores, axis=-1))
        weights = jnp.where(visible, jnp.exp(scores - new_max[..., None]), 0.0)
        new_sum = jnp.sum(weights, axis=-1)
        new_accum = jnp.einsum(
            "ths,shd->thd", weights, value_heads, precision=lax.Precision.HIGHEST
        )
        return (new_max, new_sum, new_accum)

    def keep_state(current):
        return current

    final_state = lax.cond(
        jnp.int32(0) <= first_row + row_count - 1, update, keep_state, start_state
    )
    attended = final_state[2] / final_state[1][..., None]
    head_normed = attended * lax.rsqrt(
        jnp.mean(attended * attended, axis=-1, keepdims=True) + epsilon
    )
    mixed = (head_normed[:, :, None, :] * att_weight[..., None]).reshape(
        row_count, HEADS * ATT_EXP * HDIM
    )
    mixed = mixed.astype(jnp.bfloat16)
    att_result = jnp.dot(
        mixed,
        lax.all_gather(att_out, "inner", axis=1, tiled=True),
        preferred_element_type=jnp.float32,
    )
    hidden_state = tokens.astype(jnp.float32) + att_result
    mlp_in = rms_norm(hidden_state, mlp_gain).astype(jnp.bfloat16)
    logits = jnp.dot(mlp_in, mlp_router, preferred_element_type=jnp.float32)
    expert_total = mlp_router.shape[1]
    picked = (mlp_ids[..., None] == jnp.arange(expert_total)[None, None, :]).astype(jnp.float32)
    gates = jax.nn.sigmoid(jnp.sum(picked * logits[:, None, :], axis=-1))
    outer_count = lax.axis_size("outer")
    inner_count = lax.axis_size("inner")
    device_count = outer_count * inner_count
    local_experts = w_up.shape[0]
    capacity = row_count * MLP_TOP * 5 // (4 * expert_total)
    flat_ids = mlp_ids.reshape(-1)
    one_hot = (flat_ids[:, None] == jnp.arange(expert_total)[None, :]).astype(jnp.int32)
    earlier = jnp.cumsum(one_hot, axis=0) - one_hot
    place_in_expert = jnp.sum(earlier * one_hot, axis=1)
    owner_device = flat_ids // local_experts
    owner_slot = flat_ids % local_experts
    slot_index = (owner_device * capacity + place_in_expert) * local_experts + owner_slot
    token_of_slot = jnp.full((device_count * capacity * local_experts,), row_count, jnp.int32)
    token_of_slot = token_of_slot.at[slot_index].set(jnp.arange(row_count * MLP_TOP) // MLP_TOP)
    padded_rows = jnp.concatenate([mlp_in, jnp.zeros((1, D), jnp.bfloat16)], axis=0)
    outgoing = padded_rows[token_of_slot].reshape(device_count, capacity, local_experts, D)
    hidden = jnp.einsum(
        "scej,ejh->sceh",
        lax.all_to_all(outgoing, ("outer", "inner"), split_axis=0, concat_axis=0, tiled=True),
        w_up,
        preferred_element_type=jnp.float32,
    )
    hidden = jnp.maximum(hidden, 0.0).astype(jnp.bfloat16)
    returned = lax.all_to_all(
        jnp.einsum("sceh,ehj->scej", hidden, w_down, preferred_element_type=jnp.float32).astype(
            jnp.bfloat16
        ),
        ("outer", "inner"),
        split_axis=0,
        concat_axis=0,
        tiled=True,
    )
    result_rows = returned.reshape(-1, D)[slot_index].reshape(row_count, MLP_TOP, D)
    mlp_out = jnp.sum(gates[..., None] * result_rows.astype(jnp.float32), axis=1)
    return (hidden_state + mlp_out).astype(jnp.bfloat16)


def solution(mesh):
    in_specs = (
        P(("seq", "outer", "inner"), None),
        P(("seq", "outer", "inner"), None, None),
        P(("seq", "outer", "inner"), None),
        P(),
        P("inner", None),
        P("inner", None),
        P(None, "inner"),
        P(),
        P(),
        P(("outer", "inner"), None, None),
        P(("outer", "inner"), None, None),
    )
    out_specs = P(("seq", "outer", "inner"), None)
    return jax.shard_map(
        on_device, mesh=mesh, in_specs=in_specs, out_specs=out_specs, check_vma=False
    )
```

profile of v0, /device:TPU:65, one launch (start us, length us, event | category | flops | bytes accessed | tf_op | source)
XLA Modules:
  0.0 937.8 jit_solution(16237632494527740651)
XLA Ops:
  6.5 0.7 all-gather.5.cloned.1.call-update
  7.3 1.5 fusion.14
  8.9 123.5 %all-gather.5.cloned.1.call-done = bf16[4096,768]{1,0:T(8,128)(2,1)} async-done(((bf16[1024,768]{1,0:T(8,128)(2,1)}), bf16[4096,768]{1,0:T(8,128)(2,1)}) %all-gather.5.cloned.1.call-update) | async-done | bytes 6291472 | tf_op jit(solution)/shard_map/all_gather | solution.py:41
  132.4 4.2 fusion.44
  136.6 0.6 slice.28
  137.3 10.8 %all_gather.17 = bf16[4096,8]{0,1:T(8,128)(2,1)S(1)} all-gather(bf16[1024,8]{0,1:T(8,128)(2,1)S(1)} %copy-done.8), channel_id=1, replica_groups=mesh['seq'=8,'outer'=8,'inner'=4] {'inner'}, dimensions={0}, use_global_device_ids=true | all-gather | bytes 81920 | tf_op jit(solution)/shard_map/all_gather | solution.py:46
  148.7 0.6 multiply_reduce_fusion.1
  150.4 18.0 %reduce-window.6 = s32[64,8,128]{2,1,0:T(8,128)S(1)} reduce-window(s32[64,8,128]{2,1,0:T(8,128)S(1)} %fusion.36, s32[]{:T(128)} %constant.87.clone.1), window={size=1x1x128 pad=0_0x0_0x127_0}, to_apply=%region_10.11 | reduce-window | flops 8323072 | bytes 524292 | tf_op jit(solution)/shard_map/reduce-window
  169.1 4.8 scatter_custom_fusion
  173.9 13.2 %all-gather.7.cloned.1.call-done = bf16[4096,128]{1,0:T(8,128)(2,1)} async-done(((bf16[128,128]{1,0:T(8,128)(2,1)}), bf16[4096,128]{1,0:T(8,128)(2,1)}) %all-gather.7.cloned.1.call-update) | async-done | bytes 1048592 | tf_op jit(solution)/shard_map/all_gather | solution.py:69
  187.1 52.0 %all-gather.9.cloned.1.call-done = bf16[4096,128]{0,1:T(8,128)(2,1)} async-done(((bf16[128,128]{0,1:T(8,128)(2,1)}), bf16[4096,128]{0,1:T(8,128)(2,1)}) %all-gather.9.cloned.1.call-update) | async-done | bytes 1048592 | tf_op jit(solution)/shard_map/all_gather | solution.py:70
  239.1 6.6 conditional.1
  239.6 1.5 copy.102
  241.1 1.2 fusion.43
  242.3 2.5 fusion.7
  244.8 0.8 fusion.3
  245.8 79.4 %all-gather.11.cloned.1.call-done = bf16[512,4096]{1,0:T(8,128)(2,1)} async-done(((bf16[512,1024]{1,0:T(8,128)(2,1)}), bf16[512,4096]{1,0:T(8,128)(2,1)}) %all-gather.11.cloned.1.call-update) | async-done | bytes 4194320 | tf_op jit(solution)/shard_map/all_gather | solution.py:108
  325.1 3.2 multiply_reduce_fusion
  328.3 1.3 copy-done.1
  329.9 1.0 copy-done.4
  331.0 8.4 gather_fusion
  339.4 17.4 %reshape.252 = bf16[32,20,2,4096]{3,2,1,0:T(2,128)(2,1)} reshape(bf16[1280,4096]{1,0:T(8,128)(2,1)} %gather_fusion) | data formatting | bytes 20971520 | tf_op jit(solution)/shard_map/reshape | solution.py:132
  356.8 238.7 %all_to_all.10 = bf16[32,20,2,4096]{3,2,1,0:T(2,128)(2,1)S(1)} all-to-all(bf16[32,20,2,4096]{3,2,1,0:T(2,128)(2,1)} %reshape.252), channel_id=1, replica_groups=mesh['seq'=8,'outer'=8,'inner'=4] {'outer','inner'}, dimensions={0} | all-to-all | bytes 20971520 | tf_op jit(solution)/shard_map/all_to_all | solution.py:135
  595.4 11.1 %fusion.21 = bf16[32,20,2,256]{3,1,0,2:T(8,128)(2,1)} fusion(bf16[2,4096,256]{2,1,0:T(8,128)(2,1)} %param.22, bf16[32,20,2,4096]{3,2,1,0:T(2,128)(2,1)S(1)} %all_to_all.10), kind=kOutput, calls=%fused_computation.34 | convolution fusion | flops 2685009920 | bytes 15335424 | tf_op jit(solution)/shard_map/scej,ejh->sceh/dot_general | solution.py:133
  606.5 5.3 convert_bitcast_fusion
  611.8 25.4 %copy.112 = bf16[32,20,2,4096]{3,2,1,0:T(2,128)(2,1)} copy(bf16[32,20,2,4096]{3,0,1,2:T(8,128)(2,1)S(1)} %convert_bitcast_fusion) | data formatting | bytes 20971520 | tf_op jit(solution)/shard_map/convert_element_type | solution.py:141
  637.2 6.7 all-to-all-start.1
  644.7 233.8 %all-to-all-done.1 = bf16[32,20,2,4096]{3,2,1,0:T(2,128)(2,1)} async-done(((bf16[32,20,2,4096]{3,2,1,0:T(2,128)(2,1)}), bf16[32,20,2,4096]{3,2,1,0:T(2,128)(2,1)}, u32[]{:S(2)}, u32[]{:S(2)}) %all-to-all-start.1) | async-done | bytes 10485792 | tf_op jit(solution)/shard_map/all_to_all | solution.py:140
  878.5 16.0 %reshape.253 = bf16[1280,4096]{1,0:T(8,128)(2,1)} reshape(bf16[32,20,2,4096]{3,2,1,0:T(2,128)(2,1)} %all-to-all-done.1) | data formatting | bytes 20971520 | tf_op jit(solution)/shard_map/reshape | solution.py:149
  894.6 20.4 %gather_fusion.1 = bf16[1024,4096]{1,0:T(8,128)(2,1)} fusion(bf16[1280,4096]{1,0:T(8,128)(2,1)} %reshape.253, s32[1024]{0:T(1024)S(1)} %broadcast_clamp_fusion), kind=kCustom, calls=%fused_computation.1 | custom fusion | bytes 16781312 | tf_op jit(solution)/shard_map/gather | solution.py:149
  914.9 13.3 %fusion.9 = f32[128,4096]{1,0:T(8,128)} fusion(bf16[1024,4096]{1,0:T(8,128)(2,1)} %gather_fusion.1, f32[128,8]{1,0:T(8,128)S(1)} %copy.104), kind=kLoop, calls=%fused_computation.18 | loop fusion | flops 12058624 | bytes 10489856 | tf_op jit(solution)/shard_map/reduce_sum | solution.py:150
  928.3 2.8 add_convert_fusion
  (69 shorter events, 4.1 us)
Async XLA Ops:
  6.5 637.5 %copy-start = (bf16[4096,64]{0,1:T(8,128)(2,1)S(1)}, bf16[4096,64]{0,1:T(8,128)(2,1)}, u32[]{:S(2)}) copy-start(bf16[4096,64]{0,1:T(8,128)(2,1)} %param.21) | copy-start | bytes 1572868
  6.5 125.8 %all-gather.5.cloned.1.call-start = ((), (), s32[]{:S(2)}) async-start(), calls=%async_computation.2 | async-start | bytes 7864320 | tf_op jit(solution)/shard_map/all_gather | solution.py:41
  7.3 179.8 %all-gather.7.cloned.1.call-start = ((), (), s32[]{:S(2)}) async-start(), calls=%async_computation.3 | async-start | bytes 1081344 | tf_op jit(solution)/shard_map/all_gather | solution.py:69
  8.8 128.4 %copy-start.8 = (bf16[1024,8]{0,1:T(8,128)(2,1)S(1)}, bf16[1024,8]{0,1:T(8,128)(2,1)}, u32[]{:S(2)}) copy-start(bf16[1024,8]{0,1:T(8,128)(2,1)} %param.18) | copy-start | bytes 49156
  8.8 139.2 %copy-start.10 = (s32[128,2,2]{0,2,1:T(2,128)S(1)}, s32[128,2,2]{0,2,1:T(2,128)}, u32[]{:S(2)}) copy-start(s32[128,2,2]{0,2,1:T(2,128)} %param.14) | copy-start | bytes 6148
  8.8 139.2 %copy-start.3 = (bf16[128,4096]{1,0:T(8,128)(2,1)S(1)}, bf16[128,4096]{1,0:T(8,128)(2,1)}, u32[]{:S(2)}) copy-start(bf16[128,4096]{1,0:T(8,128)(2,1)} %param.13) | copy-start | bytes 3145732
  8.9 139.2 %copy-start.6 = (f32[4096]{0:T(1024)S(1)}, f32[4096]{0:T(1024)}, u32[]{:S(2)}) copy-start(f32[4096]{0:T(1024)} %param.16) | copy-start | bytes 49156
  136.5 13.4 %copy-start.9 = (s32[128,8]{0,1:T(8,128)S(1)}, s32[128,8]{0,1:T(8,128)}, u32[]{:S(2)}) copy-start(s32[128,8]{0,1:T(8,128)} %param.15) | copy-start | bytes 12292
  137.2 101.9 %all-gather.9.cloned.1.call-start = ((), (), s32[]{:S(2)}) async-start(), calls=%async_computation.4 | async-start | bytes 1081344 | tf_op jit(solution)/shard_map/all_gather | solution.py:70
  149.4 175.8 %all-gather.11.cloned.1.call-start = ((), (), s32[]{:S(2)}) async-start(), calls=%async_computation.5 | async-start | bytes 5242880 | tf_op jit(solution)/shard_map/all_gather | solution.py:108
  241.1 1.2 copy-start.11
  325.1 4.5 copy-start.7
  328.3 1.3 copy-start.1
  329.9 1.0 copy-start.4
  637.2 6.8 copy-start.5
  637.2 241.3 %all-to-all-start.1 = ((bf16[32,20,2,4096]{3,2,1,0:T(2,128)(2,1)}), bf16[32,20,2,4096]{3,2,1,0:T(2,128)(2,1)}, u32[]{:S(2)}, u32[]{:S(2)}) async-start(bf16[32,20,2,4096]{3,2,1,0:T(2,128)(2,1)} %copy.112), calls=%async_computation.1 | async-start | bytes 20971520 | tf_op jit(solution)/shard_map/all_to_all | solution.py:140
  914.9 13.3 %copy-start.2 = (f32[128,4096]{1,0:T(8,128)S(1)}, f32[128,4096]{1,0:T(8,128)}, u32[]{:S(2)}) copy-start(f32[128,4096]{1,0:T(8,128)} %copy-done.1) | copy-start | bytes 6291460
Sparse Core Ops, SparseCore 0:
  9.2 123.1 all-gather.4
  137.3 49.7 all-gather.6
  189.5 49.4 all-gather.8
  240.7 84.3 all-gather.10
where the time goes:
time: 942 us; the launch traced here: 938 us
  waiting for transfers between devices  503 us (53%)
  blocking collectives  249 us (26%)
  local copies, waits for them, and re-layouts  98.1 us (10%)
  other arithmetic  38.2 us (4%)
  matrix products  28.3 us (3%)
  between operations  13.7 us (1%)
    all_to_all x1, blocking collectives, on_device(): lax.all_to_all(outgoing, ('outer', 'inner'), split_axis=0, concat_axis=0,...  239 us
    all_to_all x1, waiting for transfers between devices, on_device(): lax.all_to_all(jnp.einsum('sceh,ehj->scej', hidden, w_down, preferred_ele...  234 us
    all_gather x1, waiting for transfers between devices, on_device(): lax.all_gather(att_in, 'inner', axis=0, tiled=True)  123 us
    all_gather x1, waiting for transfers between devices, on_device(): lax.all_gather(att_out, 'inner', axis=1, tiled=True)  79.4 us
    all_gather x1, waiting for transfers between devices, on_device(): value_piece = lax.all_gather(values, ('outer', 'inner'), axis=0, tiled=True)  52 us
    convert_element_type x1, local copies, waits for them, and re-layouts, on_device(): jnp.einsum('sceh,ehj->scej', hidden, w_down, preferred_element_type=jnp.f...  25.4 us
    gather x1, local copies, waits for them, and re-layouts, on_device(): returned.reshape(-1, D)[slot_index].reshape(row_count, MLP_TOP, D)  20.4 us
  transfers between devices with their start and end apart: 5, of which 5 were waited for; matrix products, arithmetic and copies ran while one was open for 4% of the time, Pallas kernels for 0%

commit v1 on v0

--- a/solution.py
+++ b/solution.py
@@ -67,7 +67,12 @@
         jnp.zeros((row_count, HEADS, HDIM), jnp.float32),
     )
     key_piece = lax.all_gather(keys, ("outer", "inner"), axis=0, tiled=True)
-    value_piece = lax.all_gather(values, ("outer", "inner"), axis=0, tiled=True)
+    value_piece = jnp.concatenate(
+        lax.all_to_all(
+            jnp.stack([values] * lax.axis_size(("outer", "inner"))), ("outer", "inner"), 0, 0
+        ),
+        axis=0,
+    )
     piece_rows = key_piece.shape[0]
 
     def update(current):

time: 942 us -> 900 us (0.955)
  waiting for transfers between devices: 503 us -> 445 us
  starting transfers between devices: 6.86 us -> 17.2 us
    all_gather x1 -> x0, waiting for transfers between devices: 52 us -> none  [on_device(): value_piece = lax.all_gather(values, ('outer', 'inner'), axis=0, tiled=True)]
    all_to_all x0 -> x1, starting transfers between devices: none -> 10.4 us  [on_device(): lax.all_to_all(jnp.stack([values] * lax.axis_size(('outer', 'inner'))), (...]
  transfers between devices with their start and end apart: 5 -> 5, of which waited for: 5 -> 4; matrix products, arithmetic and copies ran while one was open for 4% -> 4% of each run, Pallas kernels for 0% -> 0%
where the time goes in v1:
time: 900 us; the launch traced here: 895 us
  waiting for transfers between devices  445 us (49%)
  blocking collectives  249 us (28%)
  local copies, waits for them, and re-layouts  103 us (11%)
  other arithmetic  37.6 us (4%)
  matrix products  28.4 us (3%)
  starting transfers between devices  17.2 us (2%)
  between operations  13.7 us (2%)
    all_to_all x1, blocking collectives, on_device(): lax.all_to_all(outgoing, ('outer', 'inner'), split_axis=0, concat_axis=0,...  239 us
    all_to_all x1, waiting for transfers between devices, on_device(): lax.all_to_all(jnp.einsum('sceh,ehj->scej', hidden, w_down, preferred_ele...  234 us
    all_gather x1, waiting for transfers between devices, on_device(): lax.all_gather(att_in, 'inner', axis=0, tiled=True)  123 us
    all_gather x1, waiting for transfers between devices, on_device(): lax.all_gather(att_out, 'inner', axis=1, tiled=True)  75.7 us
    convert_element_type x1, local copies, waits for them, and re-layouts, on_device(): jnp.einsum('sceh,ehj->scej', hidden, w_down, preferred_element_type=jnp.f...  25.4 us
    gather x1, local copies, waits for them, and re-layouts, on_device(): returned.reshape(-1, D)[slot_index].reshape(row_count, MLP_TOP, D)  20.4 us
    another operation x3, other arithmetic  18.2 us
  transfers between devices with their start and end apart: 5, of which 4 were waited for; matrix products, arithmetic and copies ran while one was open for 4% of the time, Pallas kernels for 0%

profile of v1, /device:TPU:65, one launch (start us, length us, event | category | flops | bytes accessed | tf_op | source)
XLA Modules:
  0.0 895.0 jit_solution(10702578713197618264)
XLA Ops:
  7.3 1.5 fusion.14
  8.9 123.5 %all-gather.4.cloned.1.call-done = bf16[4096,768]{1,0:T(8,128)(2,1)} async-done(((bf16[1024,768]{1,0:T(8,128)(2,1)}), bf16[4096,768]{1,0:T(8,128)(2,1)}) %all-gather.4.cloned.1.call-update) | async-done | bytes 6291472 | tf_op jit(solution)/shard_map/all_gather | solution.py:41
  132.4 4.2 fusion.44
  137.9 10.8 %all_gather.14 = bf16[4096,8]{0,1:T(8,128)(2,1)S(1)} all-gather(bf16[1024,8]{0,1:T(8,128)(2,1)S(1)} %copy-done.9), channel_id=1, replica_groups=mesh['seq'=8,'outer'=8,'inner'=4] {'inner'}, dimensions={0}, use_global_device_ids=true | all-gather | bytes 81920 | tf_op jit(solution)/shard_map/all_gather | solution.py:46
  149.4 1.2 stack.3
  150.6 10.4 %all-to-all-start = ((bf16[32,128,128]{1,2,0:T(8,128)(2,1)}), bf16[32,128,128]{1,2,0:T(8,128)(2,1)S(1)}, u32[]{:S(2)}, u32[]{:S(2)}) async-start(bf16[32,128,128]{1,2,0:T(8,128)(2,1)} %stack.3), calls=%async_computation | async-start | bytes 2097152 | tf_op jit(solution)/shard_map/all_to_all | solution.py:71
  161.4 18.0 %reduce-window.6 = s32[64,8,128]{2,1,0:T(8,128)S(1)} reduce-window(s32[64,8,128]{2,1,0:T(8,128)S(1)} %fusion.36, s32[]{:T(128)} %constant.87.clone.1), window={size=1x1x128 pad=0_0x0_0x127_0}, to_apply=%region_10.11 | reduce-window | flops 8323072 | bytes 524292 | tf_op jit(solution)/shard_map/reduce-window
  180.1 4.8 scatter_custom_fusion
  184.9 11.0 %all-gather.6.cloned.1.call-done = bf16[4096,128]{1,0:T(8,128)(2,1)} async-done(((bf16[128,128]{1,0:T(8,128)(2,1)}), bf16[4096,128]{1,0:T(8,128)(2,1)}) %all-gather.6.cloned.1.call-update) | async-done | bytes 1048592 | tf_op jit(solution)/shard_map/all_gather | solution.py:69
  195.9 10.5 %conditional.1 = (f32[128,2]{0,1:T(2,128)S(1)}, f32[128,2,64]{0,2,1:T(8,128)S(1)}) conditional(s32[]{:T(128)} %convert_element_type.63, () %tuple.13, (s32[]{:T(128)}, s32[128]{0:T(128)S(1)}, bf16[4096,128]{1,0:T(8,128)(2,1)}, bf16[128,768]{1,0:T(8,128)(2,1)S(1)}, bf16[32,128,128]{1,2,0:T(8,128)(2,1)S(1)}) %tuple.14), branch_computations={%region_3.0_spmd, %region_4.7_spmd} | conditional | flops 948436864 | bytes 27827760 | solution.py:100
  195.9 1.6 copy.108
  197.6 2.3 reshape_reshape.2
  200.4 1.5 copy.106
  201.9 1.2 fusion.43
  203.2 2.5 fusion.7
  205.6 0.8 fusion.3
  206.6 75.7 %all-gather.8.cloned.1.call-done = bf16[512,4096]{1,0:T(8,128)(2,1)} async-done(((bf16[512,1024]{1,0:T(8,128)(2,1)}), bf16[512,4096]{1,0:T(8,128)(2,1)}) %all-gather.8.cloned.1.call-update) | async-done | bytes 4194320 | tf_op jit(solution)/shard_map/all_gather | solution.py:113
  282.3 3.2 multiply_reduce_fusion
  285.5 1.3 copy-done.1
  287.1 1.0 copy-done.4
  288.2 8.4 gather_fusion
  296.6 17.4 %reshape.250 = bf16[32,20,2,4096]{3,2,1,0:T(2,128)(2,1)} reshape(bf16[1280,4096]{1,0:T(8,128)(2,1)} %gather_fusion) | data formatting | bytes 20971520 | tf_op jit(solution)/shard_map/reshape | solution.py:137
  314.0 238.7 %all_to_all.15 = bf16[32,20,2,4096]{3,2,1,0:T(2,128)(2,1)S(1)} all-to-all(bf16[32,20,2,4096]{3,2,1,0:T(2,128)(2,1)} %reshape.250), channel_id=1, replica_groups=mesh['seq'=8,'outer'=8,'inner'=4] {'outer','inner'}, dimensions={0} | all-to-all | bytes 20971520 | tf_op jit(solution)/shard_map/all_to_all | solution.py:140
  552.6 11.1 %fusion.21 = bf16[32,20,2,256]{3,1,0,2:T(8,128)(2,1)} fusion(bf16[2,4096,256]{2,1,0:T(8,128)(2,1)} %param.22, bf16[32,20,2,4096]{3,2,1,0:T(2,128)(2,1)S(1)} %all_to_all.15), kind=kOutput, calls=%fused_computation.34 | convolution fusion | flops 2685009920 | bytes 15335424 | tf_op jit(solution)/shard_map/scej,ejh->sceh/dot_general | solution.py:138
  563.7 5.3 convert_bitcast_fusion
  569.0 25.4 %copy.117 = bf16[32,20,2,4096]{3,2,1,0:T(2,128)(2,1)} copy(bf16[32,20,2,4096]{3,0,1,2:T(8,128)(2,1)S(1)} %convert_bitcast_fusion) | data formatting | bytes 20971520 | tf_op jit(solution)/shard_map/convert_element_type | solution.py:146
  594.4 6.7 all-to-all-start.2
  601.9 233.8 %all-to-all-done.2 = bf16[32,20,2,4096]{3,2,1,0:T(2,128)(2,1)} async-done(((bf16[32,20,2,4096]{3,2,1,0:T(2,128)(2,1)}), bf16[32,20,2,4096]{3,2,1,0:T(2,128)(2,1)}, u32[]{:S(2)}, u32[]{:S(2)}) %all-to-all-start.2) | async-done | bytes 10485792 | tf_op jit(solution)/shard_map/all_to_all | solution.py:145
  835.7 16.0 %reshape.251 = bf16[1280,4096]{1,0:T(8,128)(2,1)} reshape(bf16[32,20,2,4096]{3,2,1,0:T(2,128)(2,1)} %all-to-all-done.2) | data formatting | bytes 20971520 | tf_op jit(solution)/shard_map/reshape | solution.py:154
  851.7 20.4 %gather_fusion.1 = bf16[1024,4096]{1,0:T(8,128)(2,1)} fusion(bf16[1280,4096]{1,0:T(8,128)(2,1)} %reshape.251, s32[1024]{0:T(1024)S(1)} %broadcast_clamp_fusion), kind=kCustom, calls=%fused_computation.1 | custom fusion | bytes 16781312 | tf_op jit(solution)/shard_map/gather | solution.py:154
  872.1 13.3 %fusion.9 = f32[128,4096]{1,0:T(8,128)} fusion(bf16[1024,4096]{1,0:T(8,128)(2,1)} %gather_fusion.1, f32[128,8]{1,0:T(8,128)S(1)} %copy.109), kind=kLoop, calls=%fused_computation.18 | loop fusion | flops 12058624 | bytes 10489856 | tf_op jit(solution)/shard_map/reduce_sum | solution.py:155
  885.5 2.8 add_convert_fusion
  (71 shorter events, 5.5 us)
Async XLA Ops:
  6.5 594.7 %copy-start = (bf16[4096,64]{0,1:T(8,128)(2,1)S(1)}, bf16[4096,64]{0,1:T(8,128)(2,1)}, u32[]{:S(2)}) copy-start(bf16[4096,64]{0,1:T(8,128)(2,1)} %param.21) | copy-start | bytes 1572868
  6.5 125.8 %all-gather.4.cloned.1.call-start = ((), (), s32[]{:S(2)}) async-start(), calls=%async_computation.3 | async-start | bytes 7864320 | tf_op jit(solution)/shard_map/all_gather | solution.py:41
  7.3 188.7 %all-gather.6.cloned.1.call-start = ((), (), s32[]{:S(2)}) async-start(), calls=%async_computation.4 | async-start | bytes 1081344 | tf_op jit(solution)/shard_map/all_gather | solution.py:69
  8.8 129.1 %copy-start.9 = (bf16[1024,8]{0,1:T(8,128)(2,1)S(1)}, bf16[1024,8]{0,1:T(8,128)(2,1)}, u32[]{:S(2)}) copy-start(bf16[1024,8]{0,1:T(8,128)(2,1)} %param.18) | copy-start | bytes 49156
  8.8 139.9 %copy-start.11 = (s32[128,2,2]{0,2,1:T(2,128)S(1)}, s32[128,2,2]{0,2,1:T(2,128)}, u32[]{:S(2)}) copy-start(s32[128,2,2]{0,2,1:T(2,128)} %param.14) | copy-start | bytes 6148
  8.9 139.9 %copy-start.3 = (bf16[128,4096]{1,0:T(8,128)(2,1)S(1)}, bf16[128,4096]{1,0:T(8,128)(2,1)}, u32[]{:S(2)}) copy-start(bf16[128,4096]{1,0:T(8,128)(2,1)} %param.13) | copy-start | bytes 3145732
  8.9 139.9 %copy-start.7 = (f32[4096]{0:T(1024)S(1)}, f32[4096]{0:T(1024)}, u32[]{:S(2)}) copy-start(f32[4096]{0:T(1024)} %param.16) | copy-start | bytes 49156
  136.5 24.4 %copy-start.10 = (s32[128,8]{0,1:T(8,128)S(1)}, s32[128,8]{0,1:T(8,128)}, u32[]{:S(2)}) copy-start(s32[128,8]{0,1:T(8,128)} %param.15) | copy-start | bytes 12292
  137.2 145.1 %all-gather.8.cloned.1.call-start = ((), (), s32[]{:S(2)}) async-start(), calls=%async_computation.5 | async-start | bytes 5242880 | tf_op jit(solution)/shard_map/all_gather | solution.py:113
  150.6 45.3 %all-to-all-start = ((bf16[32,128,128]{1,2,0:T(8,128)(2,1)}), bf16[32,128,128]{1,2,0:T(8,128)(2,1)S(1)}, u32[]{:S(2)}, u32[]{:S(2)}) async-start(bf16[32,128,128]{1,2,0:T(8,128)(2,1)} %stack.3), calls=%async_computation | async-start | bytes 2097152 | tf_op jit(solution)/shard_map/all_to_all | solution.py:71
  201.9 1.2 copy-start.6
  282.3 4.5 copy-start.8
  285.5 1.3 copy-start.1
  287.1 1.0 copy-start.4
  594.4 6.8 copy-start.5
  594.4 241.3 %all-to-all-start.2 = ((bf16[32,20,2,4096]{3,2,1,0:T(2,128)(2,1)}), bf16[32,20,2,4096]{3,2,1,0:T(2,128)(2,1)}, u32[]{:S(2)}, u32[]{:S(2)}) async-start(bf16[32,20,2,4096]{3,2,1,0:T(2,128)(2,1)} %copy.117), calls=%async_computation.2 | async-start | bytes 20971520 | tf_op jit(solution)/shard_map/all_to_all | solution.py:145
  872.1 13.3 %copy-start.2 = (f32[128,4096]{1,0:T(8,128)S(1)}, f32[128,4096]{1,0:T(8,128)}, u32[]{:S(2)}) copy-start(f32[128,4096]{1,0:T(8,128)} %copy-done.1) | copy-start | bytes 6291460
Sparse Core Ops, SparseCore 0:
  9.2 123.1 all-gather.3
  137.3 58.5 all-gather.5
  197.7 84.5 all-gather.7
